TPU v7x, 128 devices: a whole 4x4x4 slice. The times are simulated.
128 devices in a mesh: row: 8 (over x, core), col: 16 (over y, z).
Axes of the slice: x: 4, y: 4, z: 4, core: 2. Of those that a mesh axis runs over, the one named last changes fastest.
Arguments:
- trail: bfloat16 [16384, 16384], P('row', 'col'), may hold values from -0.046875 to 0.046875
- row_one: bfloat16 [128, 16384], P('row', 'col'), may hold values from -0.5 to 0.5
- row_two: bfloat16 [128, 16384], P('row', 'col'), may hold values from -0.5 to 0.5
- diag_one: float32 [128, 128], replicated, may hold values from -1 to 2, as said below
- diag_two: float32 [128, 128], replicated, may hold values from -1 to 2, as said below
- adj_trail: float32 [16384, 16384], P('row', 'col'), may hold values from -6 to 6
- adj_row_one: float32 [128, 16384], P('row', 'col'), may hold values from -6 to 6
- adj_row_two: float32 [128, 16384], P('row', 'col'), may hold values from -6 to 6
- adj_diag_one: float32 [128, 128], replicated, may hold values from -6 to 6
- adj_diag_two: float32 [128, 128], replicated, may hold values from -6 to 6
Outputs:
- grad_trail: bfloat16 [16384, 16384], P('row', 'col')
- grad_row_one: float32 [128, 16384], P('row', 'col')
- grad_row_two: float32 [128, 16384], P('row', 'col')
- grad_diag_one: float32 [128, 128], replicated
- grad_diag_two: float32 [128, 128], replicated
Inputs may be any that keep to these rules, and one draw needn't show every extreme that they name: `diag_one`: lower triangular with a positive diagonal. `diag_two`: lower triangular with a positive diagonal.
All inputs are finite; a program needn't handle non-finite values.
Results may differ from a plain program's by a relative error of at most 0.014.
Values may be sent and summed in bfloat16 or wider, within the bound.
A program may use at most 128 MiB of HBM per device.

v0:
```python
import jax
import jax.numpy as jnp
from jax import lax
from jax.sharding import PartitionSpec as P

exact_mode = lax.Precision.HIGHEST


def from_root(value, axis, source):
    kept = jnp.where(lax.axis_index(axis) == source, value, 0).astype(value.dtype)
    return lax.psum(kept, axis)


def halved_lower(matrix):
    order = matrix.shape[0]
    keep = jnp.tril(jnp.ones((order, order), matrix.dtype)) - 0.5 * jnp.eye(
        order, dtype=matrix.dtype
    )
    return matrix * keep


def inverse_lower(block):
    ident = jnp.eye(block.shape[0], dtype=block.dtype)
    return lax.linalg.triangular_solve(block, ident, left_side=True, lower=True)


def block_adjoint(block, inverse, seed_adj):
    inner = halved_lower(jnp.dot(block.T, seed_adj, precision=exact_mode))
    middle = jnp.dot(inverse.T, inner, precision=exact_mode)
    return halved_lower(jnp.dot(middle, inverse, precision=exact_mode))


def per_device(
    trail,
    row_one,
    row_two,
    diag_one,
    diag_two,
    adj_trail,
    adj_row_one,
    adj_row_two,
    adj_diag_one,
    adj_diag_two,
):
    panel = diag_one.shape[0]
    width = trail.shape[1]
    band = row_one.shape[0]
    last = width - panel
    col_count = lax.axis_size("col")
    col_here = lax.axis_index("col")
    row_start = lax.axis_index("row") * band
    here_one = col_here == col_count - 2
    here_two = col_here == col_count - 1
    full_one, full_two = (
        lax.all_gather(row_one, "row", axis=0, tiled=True),
        lax.all_gather(row_two, "row", axis=0, tiled=True),
    )

    def own_rows(matrix):
        return lax.dynamic_slice_in_dim(matrix, row_start, band, 0)

    def solve_panel(rows, inverse, root):
        whole = from_root(rows, "col", root)
        return jnp.dot(whole, inverse, precision=exact_mode).astype(jnp.bfloat16)

    def summed_block(partial_value, root):
        rows_sum = lax.psum(partial_value, "row")
        return from_root(rows_sum, "col", root)

    inverse_two = inverse_lower(diag_two)
    solved_two = solve_panel(adj_trail[:, last:], inverse_two, col_count - 1)
    partial_two = jnp.dot(solved_two.T, trail[:, last:], preferred_element_type=jnp.float32)
    seed_two = jnp.tril(adj_diag_two - summed_block(partial_two, col_count - 1))
    grad_diag_two = block_adjoint(diag_two, inverse_two, seed_two)
    mirror_two = own_rows(grad_diag_two + grad_diag_two.T)
    rest_two = jnp.dot(mirror_two, full_two.astype(jnp.float32), precision=exact_mode)
    inverse_one = inverse_lower(diag_one)
    crossed = lax.psum_scatter(
        jnp.dot(solved_two.T, trail, preferred_element_type=jnp.float32).astype(jnp.bfloat16),
        "row",
        scatter_dimension=0,
        tiled=True,
    ).astype(jnp.float32)
    adj_two = adj_row_two - crossed - rest_two
    adj_next = adj_trail - jnp.dot(solved_two, full_two, preferred_element_type=jnp.float32)
    stacked = jnp.concatenate([adj_two[:, last:], adj_next[:, last:]], 0)
    solved_one = solve_panel(stacked, inverse_one, col_count - 2)
    head_rows = solved_one[:band]
    tail_rows = solved_one[band:]
    partial_one = jnp.dot(
        head_rows.T, row_two[:, last:], preferred_element_type=jnp.float32
    ) + jnp.dot(tail_rows.T, trail[:, last:], preferred_element_type=jnp.float32)
    seed_one = jnp.tril(adj_diag_one - summed_block(partial_one, col_count - 2))
    grad_diag_one = block_adjoint(diag_one, inverse_one, seed_one)
    mirror_one = own_rows(grad_diag_one + grad_diag_one.T)
    rest_one = jnp.dot(mirror_one, full_one.astype(jnp.float32), precision=exact_mode)
    head_update = jnp.dot(head_rows, full_one, preferred_element_type=jnp.float32)
    two_left = adj_two - head_update
    trail_left = adj_next - jnp.dot(tail_rows, full_one, preferred_element_type=jnp.float32)
    crossed_one = lax.psum_scatter(
        (
            jnp.dot(head_rows.T, row_two, preferred_element_type=jnp.float32)
            + jnp.dot(tail_rows.T, trail, preferred_element_type=jnp.float32)
        ).astype(jnp.bfloat16),
        "row",
        scatter_dimension=0,
        tiled=True,
    ).astype(jnp.float32)
    one_left = adj_row_one - crossed_one - rest_one
    trail_block = jnp.where(
        here_one,
        tail_rows.astype(jnp.float32),
        jnp.where(here_two, solved_two.astype(jnp.float32), trail_left[:, last:]),
    )
    grad_trail = jnp.concatenate([trail_left[:, :last], trail_block], 1).astype(jnp.bfloat16)
    zero_block = jnp.zeros((band, panel), jnp.float32)
    one_block = jnp.where(here_one | here_two, zero_block, one_left[:, last:])
    grad_row_one = jnp.concatenate([one_left[:, :last], one_block], 1)
    two_block = jnp.where(
        here_one, head_rows.astype(jnp.float32), jnp.where(here_two, zero_block, two_left[:, last:])
    )
    grad_row_two = jnp.concatenate([two_left[:, :last], two_block], 1)
    return (grad_trail, grad_row_one, grad_row_two, grad_diag_one, grad_diag_two)


def solution(mesh):
    in_specs = (
        P("row", "col"),
        P("row", "col"),
        P("row", "col"),
        P(),
        P(),
        P("row", "col"),
        P("row", "col"),
        P("row", "col"),
        P(),
        P(),
    )
    out_specs = (P("row", "col"), P("row", "col"), P("row", "col"), P(), P())
    return jax.shard_map(
        per_device, mesh=mesh, in_specs=in_specs, out_specs=out_specs, check_vma=False
    )
```

profile of v0, /device:TPU:0, one launch (start us, length us, event | category | flops | bytes accessed | tf_op | source)
XLA Modules:
  0.0 564.0 jit_solution(18032866646956129577)
XLA Ops:
  7.2 0.0 all-reduce.7.cloned.1.call-start
  7.2 2.3 slice_select_fusion.1
  9.5 0.0 all-reduce.7.cloned.1.call-update
  9.5 0.0 all-reduce.9.cloned.1.call-start
  9.6 0.9 select_bitcast_fusion.1
  10.4 9.8 %custom-call.4 = f32[1,128,128]{1,2,0:T(8,128)S(1)} custom-call(f32[1,128,128]{2,1,0:T(8,128)S(1)} %select_bitcast_fusion.1), custom_call_target="InvertDiagBlocksLowerTriangular" | custom-call | tf_op jit(solution)/shard_map/triangular_solve/custom-call.1 | solution.py:24
  20.3 13.5 %all_gather.6 = bf16[128,1024]{1,0:T(8,128)(2,1)S(1)} all-gather(bf16[16,1024]{1,0:T(8,128)(2,1)} %param.14), channel_id=1, replica_groups=mesh['row'=8,'col'=16] {'row'}, dimensions={0}, use_global_device_ids=true | all-gather | bytes 294912 | tf_op jit(solution)/shard_map/all_gather | solution.py:56
  33.7 0.3 fusion.13
  34.0 67.5 %all-reduce.7.cloned.1.call-done = f32[2048,128]{1,0:T(8,128)} async-done(((f32[2048,128]{1,0:T(8,128)}), f32[2048,128]{1,0:T(8,128)}) %all-reduce.7.cloned.1.call-update) | async-done | bytes 1048592 | tf_op jit(solution)/shard_map/psum | solution.py:11
  101.5 2.2 convolution_convert_fusion.1
  103.7 2.0 fusion.6
  105.7 0.0 all-reduce.9.cloned.1.call-update
  105.7 0.0 all-reduce.11.cloned.1.call-start
  105.8 7.9 %convolution_subtract_fusion.1 = f32[2048,1024]{1,0:T(8,128)} fusion(f32[2048,1024]{1,0:T(8,128)} %param.17, bf16[2048,128]{1,0:T(8,128)(2,1)S(1)} %convolution_convert_fusion.1, bf16[128,1024]{1,0:T(8,128)(2,1)S(1)} %all_gather.6), kind=kOutput, calls=%fused_computation.2 | convolution fusion | flops 538968064 | bytes 17563648 | tf_op jit(solution)/shard_map/dot_general | solution.py:85
  113.6 50.0 %all-reduce.9.cloned.1.call-done = f32[128,128]{1,0:T(8,128)} async-done(((f32[128,128]{1,0:T(8,128)}), f32[128,128]{1,0:T(8,128)}) %all-reduce.9.cloned.1.call-update) | async-done | bytes 65552 | tf_op jit(solution)/shard_map/psum | solution.py:67
  163.6 0.6 broadcast_select_fusion.1
  164.2 0.0 all-reduce.11.cloned.1.call-update
  164.3 0.0 reduce-scatter.7.cloned.1.call-start
  164.3 3.7 convolution_convert_fusion.2
  168.0 0.0 reduce-scatter.7.cloned.1.call-update
  168.1 0.0 all-reduce.13.cloned.1.call-start
  168.1 79.6 %all-reduce.11.cloned.1.call-done = f32[128,128]{1,0:T(8,128)} async-done(((f32[128,128]{1,0:T(8,128)}), f32[128,128]{1,0:T(8,128)}) %all-reduce.11.cloned.1.call-update) | async-done | bytes 65552 | tf_op jit(solution)/shard_map/psum | solution.py:11
  247.7 1.1 fusion.2
  248.9 0.3 fusion.42
  249.2 0.2 fusion.25
  249.4 0.1 copy.62
  249.5 30.7 %reduce-scatter.7.cloned.1.call-done = bf16[16,1024]{1,0:T(8,128)(2,1)} async-done(((bf16[128,1024]{1,0:T(8,128)(2,1)}), bf16[16,1024]{1,0:T(8,128)(2,1)}) %reduce-scatter.7.cloned.1.call-update) | async-done | bytes 32784 | tf_op jit(solution)/shard_map/reduce_scatter | solution.py:78
  280.2 1.0 convolution_subtract_fusion.4
  281.2 1.0 maximum_select_fusion
  282.3 0.0 all-reduce.13.cloned.1.call-update
  282.3 0.0 all-reduce.15.cloned.1.call-start
  282.4 9.8 %custom-call.5 = f32[1,128,128]{1,2,0:T(8,128)S(1)} custom-call(f32[1,128,128]{2,1,0:T(8,128)S(1)} %select_bitcast_fusion), custom_call_target="InvertDiagBlocksLowerTriangular" | custom-call | tf_op jit(solution)/shard_map/triangular_solve/custom-call.1 | solution.py:24
  292.2 13.0 %all_gather.7 = bf16[128,1024]{1,0:T(8,128)(2,1)S(1)} all-gather(bf16[16,1024]{1,0:T(8,128)(2,1)S(1)} %copy-done.10), channel_id=1, replica_groups=mesh['row'=8,'col'=16] {'row'}, dimensions={0}, use_global_device_ids=true | all-gather | bytes 294912 | tf_op jit(solution)/shard_map/all_gather | solution.py:55
  305.2 0.3 fusion.11
  305.5 64.7 %all-reduce.13.cloned.1.call-done = f32[2064,128]{1,0:T(8,128)} async-done(((f32[2064,128]{1,0:T(8,128)}), f32[2064,128]{1,0:T(8,128)}) %all-reduce.13.cloned.1.call-update) | async-done | bytes 1056784 | tf_op jit(solution)/shard_map/psum | solution.py:11
  370.2 2.2 convolution_convert_fusion
  372.4 0.2 fusion.32
  372.6 0.2 fusion.36
  372.8 0.2 convolution_subtract_fusion.2
  373.0 6.7 %convolution_subtract_fusion = bf16[2048,1024]{1,0:T(8,128)(2,1)} fusion(f32[2048,1024]{1,0:T(8,128)} %convolution_subtract_fusion.1, bf16[128,1024]{1,0:T(8,128)(2,1)S(1)} %all_gather.7, bf16[2064,128]{1,0:T(8,128)(2,1)S(1)} %convolution_convert_fusion), kind=kOutput, calls=%fused_computation.1 | convolution fusion | flops 541065216 | bytes 13369344 | tf_op jit(solution)/shard_map/dot_general | solution.py:99
  379.7 2.0 convolution_add_fusion.1
  381.7 0.0 all-reduce.15.cloned.1.call-update
  381.7 0.0 all-reduce.17.cloned.1.call-start
  381.7 3.6 fusion
  385.4 1.2 fusion.4
  386.6 0.0 slice-start.1
  386.7 4.1 slice.97
  390.8 48.5 %all-reduce.15.cloned.1.call-done = f32[128,128]{1,0:T(8,128)} async-done(((f32[128,128]{1,0:T(8,128)}), f32[128,128]{1,0:T(8,128)}) %all-reduce.15.cloned.1.call-update) | async-done | bytes 65552 | tf_op jit(solution)/shard_map/psum | solution.py:67
  439.3 0.6 broadcast_select_fusion
  439.9 0.0 all-reduce.17.cloned.1.call-update
  440.0 0.0 reduce-scatter.9.cloned.1.call-start
  440.0 0.6 pad_maximum_fusion.2
  440.6 0.0 reduce-scatter.9.cloned.1.call-update
  440.7 0.0 copy-start.8
  440.7 0.0 copy-start.9
  440.7 4.7 pad_maximum_fusion
  445.4 78.0 %all-reduce.17.cloned.1.call-done = f32[128,128]{1,0:T(8,128)} async-done(((f32[128,128]{1,0:T(8,128)}), f32[128,128]{1,0:T(8,128)}) %all-reduce.17.cloned.1.call-update) | async-done | bytes 65552 | tf_op jit(solution)/shard_map/psum | solution.py:11
  523.4 1.1 fusion.1
  524.6 0.3 fusion.43
  524.8 0.2 fusion.24
  525.1 0.1 copy.67
  525.2 30.3 %reduce-scatter.9.cloned.1.call-done = bf16[16,1024]{1,0:T(8,128)(2,1)} async-done(((bf16[128,1024]{1,0:T(8,128)(2,1)}), bf16[16,1024]{1,0:T(8,128)(2,1)}) %reduce-scatter.9.cloned.1.call-update) | async-done | bytes 32784 | tf_op jit(solution)/shard_map/reduce_scatter | solution.py:100
  555.5 1.0 convolution_subtract_fusion.3
  556.5 0.6 pad_maximum_fusion.1
  (29 shorter events, 0.1 us)
Async XLA Ops:
  7.2 94.3 %all-reduce.7.cloned.1.call-start = ((), (), s32[]{:S(2)}) async-start(), calls=%async_computation.2 | async-start | bytes 2097152 | tf_op jit(solution)/shard_map/psum | solution.py:11
  9.5 154.1 %all-reduce.9.cloned.1.call-start = ((), (), s32[]{:S(2)}) async-start(), calls=%async_computation.3 | async-start | bytes 131072 | tf_op jit(solution)/shard_map/psum | solution.py:67
  105.7 142.0 %all-reduce.11.cloned.1.call-start = ((), (), s32[]{:S(2)}) async-start(), calls=%async_computation.4 | async-start | bytes 131072 | tf_op jit(solution)/shard_map/psum | solution.py:11
  113.6 134.1 %copy-start.1 = (f32[128,128]{1,0:T(8,128)S(1)}, f32[128,128]{1,0:T(8,128)}, u32[]{:S(2)}) copy-start(f32[128,128]{1,0:T(8,128)} %param.16) | copy-start | bytes 196612
  113.6 134.1 %copy-start.6 = (f32[128,128]{1,0:T(8,128)S(1)}, f32[128,128]{1,0:T(8,128)}, u32[]{:S(2)}) copy-start(f32[128,128]{1,0:T(8,128)} %param.21) | copy-start | bytes 196612
  113.6 166.6 %copy-start.7 = (f32[16,1024]{1,0:T(8,128)S(1)}, f32[16,1024]{1,0:T(8,128)}, u32[]{:S(2)}) copy-start(f32[16,1024]{1,0:T(8,128)} %param.19) | copy-start | bytes 196612
  164.3 117.0 %slice-start = ((f32[2048,1024]{1,0:T(8,128)}), f32[2048,128]{1,0:T(8,128)S(1)}, s32[]{:S(2)}) async-start(f32[2048,1024]{1,0:T(8,128)} %convolution_subtract_fusion.1), calls=%async_computation.10 | async-start | bytes 2097152 | tf_op jit(solution)/shard_map/slice | solution.py:86
  164.3 116.0 %reduce-scatter.7.cloned.1.call-start = ((), (), s32[]{:S(2)}) async-start(), calls=%async_computation.8 | async-start | bytes 294912 | tf_op jit(solution)/shard_map/reduce_scatter | solution.py:78
  168.0 114.3 %copy-start.2 = (f32[128,128]{1,0:T(8,128)S(1)}, f32[128,128]{1,0:T(8,128)}, u32[]{:S(2)}) copy-start(f32[128,128]{1,0:T(8,128)} %param.15) | copy-start | bytes 196612
  168.0 124.2 %copy-start.10 = (bf16[16,1024]{1,0:T(8,128)(2,1)S(1)}, bf16[16,1024]{1,0:T(8,128)(2,1)}, u32[]{:S(2)}) copy-start(bf16[16,1024]{1,0:T(8,128)(2,1)} %param.13) | copy-start | bytes 98308
  168.0 204.4 %copy-start.3 = (bf16[16,1024]{1,0:T(8,128)(2,1)S(1)}, bf16[16,1024]{1,0:T(8,128)(2,1)}, u32[]{:S(2)}) copy-start(bf16[16,1024]{1,0:T(8,128)(2,1)} %param.14) | copy-start | bytes 98308
  168.1 202.1 %all-reduce.13.cloned.1.call-start = ((), (), s32[]{:S(2)}) async-start(), calls=%async_computation.5 | async-start | bytes 2113536 | tf_op jit(solution)/shard_map/psum | solution.py:11
  249.4 130.3 %copy-start.4 = (f32[128,128]{1,0:T(8,128)}, f32[128,128]{1,0:T(8,128)S(1)}, u32[]{:S(2)}) copy-start(f32[128,128]{1,0:T(8,128)S(1)} %get-tuple-element.16) | copy-start | bytes 196612
  282.3 157.0 %all-reduce.15.cloned.1.call-start = ((), (), s32[]{:S(2)}) async-start(), calls=%async_computation.6 | async-start | bytes 131072 | tf_op jit(solution)/shard_map/psum | solution.py:67
  373.0 13.7 %copy-start = (f32[16,1024]{1,0:T(8,128)}, f32[16,1024]{1,0:T(8,128)S(1)}, u32[]{:S(2)}) copy-start(f32[16,1024]{1,0:T(8,128)S(1)} %convolution_subtract_fusion.2) | copy-start | bytes 196612
  381.7 141.7 %all-reduce.17.cloned.1.call-start = ((), (), s32[]{:S(2)}) async-start(), calls=%async_computation.7 | async-start | bytes 131072 | tf_op jit(solution)/shard_map/psum | solution.py:11
  386.6 53.4 %slice-start.1 = ((f32[16,1024]{1,0:T(8,128)}), f32[16,896]{1,0:T(8,128)S(1)}, s32[]{:S(2)}) async-start(f32[16,1024]{1,0:T(8,128)} %copy-done), calls=%async_computation.11 | async-start | bytes 114688 | tf_op jit(solution)/shard_map/slice | solution.py:122
  440.0 115.5 %reduce-scatter.9.cloned.1.call-start = ((), (), s32[]{:S(2)}) async-start(), calls=%async_computation.9 | async-start | bytes 294912 | tf_op jit(solution)/shard_map/reduce_scatter | solution.py:100
  440.7 82.7 %copy-start.8 = (f32[128,128]{1,0:T(8,128)S(1)}, f32[128,128]{1,0:T(8,128)}, u32[]{:S(2)}) copy-start(f32[128,128]{1,0:T(8,128)} %param.20) | copy-start | bytes 196612
  440.7 114.8 %copy-start.9 = (f32[16,1024]{1,0:T(8,128)S(1)}, f32[16,1024]{1,0:T(8,128)}, u32[]{:S(2)}) copy-start(f32[16,1024]{1,0:T(8,128)} %param.18) | copy-start | bytes 196612
  525.1 32.1 %copy-start.5 = (f32[128,128]{1,0:T(8,128)}, f32[128,128]{1,0:T(8,128)S(1)}, u32[]{:S(2)}) copy-start(f32[128,128]{1,0:T(8,128)S(1)} %get-tuple-element.18) | copy-start | bytes 196612
Sparse Core Ops, SparseCore 0:
  11.8 89.6 all-reduce.6
  105.8 57.6 all-reduce.8
  167.7 79.9 all-reduce.10
  250.5 29.6 reduce-scatter.6
  284.3 85.8 all-reduce.12
  381.8 57.4 all-reduce.14
  443.4 79.9 all-reduce.16
  525.8 29.6 reduce-scatter.8
where the time goes:
time: 565 us; the launch traced here: 564 us
  waiting for transfers between devices  449 us (79%)
  matrix products  36.6 us (6%)
  other arithmetic  32.3 us (6%)
  blocking collectives  26.5 us (5%)
  between operations  14.4 us (3%)
    psum x4, waiting for transfers between devices, from_root(): return lax.psum(kept, axis)  290 us
    psum x2, waiting for transfers between devices, summed_block(): rows_sum = lax.psum(partial_value, 'row')  98.4 us
    reduce_scatter x1, waiting for transfers between devices, per_device(): lax.psum_scatter(jnp.dot(solved_two.T, trail, preferred_element_type=jnp....  30.7 us
    reduce_scatter x1, waiting for transfers between devices, per_device(): lax.psum_scatter((jnp.dot(head_rows.T, row_two, preferred_element_type=jn...  30.3 us
    another operation x2, other arithmetic, inverse_lower(): return lax.linalg.triangular_solve(block, ident, left_side=True, lower=True)  19.6 us
    all_gather x1, blocking collectives, per_device(): lax.all_gather(row_two, 'row', axis=0, tiled=True)  13.5 us
    all_gather x1, blocking collectives, per_device(): lax.all_gather(row_one, 'row', axis=0, tiled=True)  13 us
  transfers between devices with their start and end apart: 8, of which 8 were waited for; matrix products, arithmetic and copies ran while one was open for 9% of the time, Pallas kernels for 0%

commit v1 on v0

--- a/solution.py
+++ b/solution.py
@@ -4,6 +4,24 @@
 from jax.sharding import PartitionSpec as P
 
 exact_mode = lax.Precision.HIGHEST
+
+
+def gather_around(shard, axis, dim):
+    ways, here, hop = (lax.axis_size(axis), lax.axis_index(axis), shard.shape[dim])
+    dims = [n * ways if d == dim else n for d, n in enumerate(shard.shape)]
+    full = lax.dynamic_update_slice_in_dim(
+        jnp.zeros(dims, shard.dtype), shard, here * hop, axis=dim
+    )
+    going_up = going_down = shard
+    for far in range(1, ways // 2 + 1):
+        going_up = lax.ppermute(going_up, axis, [(d, (d + 1) % ways) for d in range(ways)])
+        full = lax.dynamic_update_slice_in_dim(full, going_up, (here - far) % ways * hop, axis=dim)
+        if 2 * far < ways:
+            going_down = lax.ppermute(going_down, axis, [(d, (d - 1) % ways) for d in range(ways)])
+            full = lax.dynamic_update_slice_in_dim(
+                full, going_down, (here + far) % ways * hop, axis=dim
+            )
+    return full
 
 
 def from_root(value, axis, source):
@@ -52,7 +70,7 @@
     here_one = col_here == col_count - 2
     here_two = col_here == col_count - 1
     full_one, full_two = (
-        lax.all_gather(row_one, "row", axis=0, tiled=True),
+        gather_around(row_one, "row", 0),
         lax.all_gather(row_two, "row", axis=0, tiled=True),
     )
 

time: 565 us -> 565 us (level)
  blocking collectives: 26.5 us -> 13 us
  starting transfers between devices: 0.33 us -> 9.38 us
    all_gather x1 -> x0, blocking collectives: 13 us -> none  [per_device(): lax.all_gather(row_one, 'row', axis=0, tiled=True)]
    ppermute x0 -> x7, starting transfers between devices: none -> 8.87 us  [the longest x3 8.83 us: gather_around(): lax.ppermute(going_down, axis, [(d, (d - 1) % ways) for d in range(ways)])]
    ppermute x0 -> x7, waiting for transfers between devices: none -> 7.68 us  [the longest x4 7.67 us: gather_around(): lax.ppermute(going_up, axis, [(d, (d + 1) % ways) for d in range(ways)])]
  transfers between devices with their start and end apart: 8 -> 15, of which waited for: 8 -> 11; matrix products, arithmetic and copies ran while one was open for 9% -> 10% of each run, Pallas kernels for 0% -> 0%
where the time goes in v1:
time: 565 us; the launch traced here: 564 us
  waiting for transfers between devices  453 us (80%)
  matrix products  36.6 us (6%)
  other arithmetic  33.2 us (6%)
  between operations  14.6 us (3%)
  blocking collectives  13 us (2%)
  starting transfers between devices  9.38 us (2%)
    psum x4, waiting for transfers between devices, from_root(): return lax.psum(kept, axis)  285 us
    psum x2, waiting for transfers between devices, summed_block(): rows_sum = lax.psum(partial_value, 'row')  98.4 us
    reduce_scatter x1, waiting for transfers between devices, per_device(): lax.psum_scatter(jnp.dot(solved_two.T, trail, preferred_element_type=jnp....  30.7 us
    reduce_scatter x1, waiting for transfers between devices, per_device(): lax.psum_scatter((jnp.dot(head_rows.T, row_two, preferred_element_type=jn...  30.3 us
    another operation x2, other arithmetic, inverse_lower(): return lax.linalg.triangular_solve(block, ident, left_side=True, lower=True)  19.6 us
    all_gather x1, blocking collectives, per_device(): lax.all_gather(row_two, 'row', axis=0, tiled=True)  13 us
  transfers between devices with their start and end apart: 15, of which 11 were waited for; matrix products, arithmetic and copies ran while one was open for 10% of the time, Pallas kernels for 0%

profile of v1, /device:TPU:0, one launch (start us, length us, event | category | flops | bytes accessed | tf_op | source)
XLA Modules:
  0.0 563.9 jit_solution(12214027530895433746)
XLA Ops:
  7.2 0.0 all-reduce.7.cloned.1.call-start
  7.2 2.3 slice_select_fusion.1
  9.5 0.0 all-reduce.9.cloned.1.call-start
  9.6 0.0 collective-permute-start
  9.6 2.9 collective-permute-start.1
  12.5 0.8 select_bitcast_fusion.1
  13.4 9.8 %custom-call.4 = f32[1,128,128]{1,2,0:T(8,128)S(1)} custom-call(f32[1,128,128]{2,1,0:T(8,128)S(1)} %select_bitcast_fusion.1), custom_call_target="InvertDiagBlocksLowerTriangular" | custom-call | tf_op jit(solution)/shard_map/triangular_solve/custom-call.1 | solution.py:42
  23.2 0.9 select_bitcast_fusion
  24.1 9.8 %custom-call.5 = f32[1,128,128]{1,2,0:T(8,128)S(1)} custom-call(f32[1,128,128]{2,1,0:T(8,128)S(1)} %select_bitcast_fusion), custom_call_target="InvertDiagBlocksLowerTriangular" | custom-call | tf_op jit(solution)/shard_map/triangular_solve/custom-call.1 | solution.py:42
  33.9 13.0 %all_gather.3 = bf16[128,1024]{1,0:T(8,128)(2,1)S(1)} all-gather(bf16[16,1024]{1,0:T(8,128)(2,1)} %param.14), channel_id=1, replica_groups=mesh['row'=8,'col'=16] {'row'}, dimensions={0}, use_global_device_ids=true | all-gather | bytes 294912 | tf_op jit(solution)/shard_map/all_gather | solution.py:74
  46.9 0.3 fusion.13
  47.2 54.3 %all-reduce.7.cloned.1.call-done = f32[2048,128]{1,0:T(8,128)} async-done(((f32[2048,128]{1,0:T(8,128)}), f32[2048,128]{1,0:T(8,128)}) %all-reduce.7.cloned.1.call-update) | async-done | bytes 1048592 | tf_op jit(solution)/shard_map/psum | solution.py:29
  101.5 2.2 convolution_convert_fusion.1
  103.7 2.0 fusion.6
  105.7 0.0 all-reduce.11.cloned.1.call-start
  105.8 7.9 %convolution_subtract_fusion.1 = f32[2048,1024]{1,0:T(8,128)} fusion(f32[2048,1024]{1,0:T(8,128)} %param.17, bf16[2048,128]{1,0:T(8,128)(2,1)S(1)} %convolution_convert_fusion.1, bf16[128,1024]{1,0:T(8,128)(2,1)S(1)} %all_gather.3), kind=kOutput, calls=%fused_computation.2 | convolution fusion | flops 538968064 | bytes 17563648 | tf_op jit(solution)/shard_map/dot_general | solution.py:103
  113.7 49.9 %all-reduce.9.cloned.1.call-done = f32[128,128]{1,0:T(8,128)} async-done(((f32[128,128]{1,0:T(8,128)}), f32[128,128]{1,0:T(8,128)}) %all-reduce.9.cloned.1.call-update) | async-done | bytes 65552 | tf_op jit(solution)/shard_map/psum | solution.py:85
  163.6 0.6 broadcast_select_fusion.1
  164.2 0.0 all-reduce.11.cloned.1.call-update
  164.3 0.0 reduce-scatter.7.cloned.1.call-start
  164.3 3.7 convolution_convert_fusion.2
  168.0 0.0 reduce-scatter.7.cloned.1.call-update
  168.1 0.0 all-reduce.13.cloned.1.call-start
  168.1 79.6 %all-reduce.11.cloned.1.call-done = f32[128,128]{1,0:T(8,128)} async-done(((f32[128,128]{1,0:T(8,128)}), f32[128,128]{1,0:T(8,128)}) %all-reduce.11.cloned.1.call-update) | async-done | bytes 65552 | tf_op jit(solution)/shard_map/psum | solution.py:29
  247.7 1.1 fusion.2
  248.9 0.3 fusion.42
  249.2 0.2 fusion.25
  249.4 0.1 copy.62
  249.5 30.7 %reduce-scatter.7.cloned.1.call-done = bf16[16,1024]{1,0:T(8,128)(2,1)} async-done(((bf16[128,1024]{1,0:T(8,128)(2,1)}), bf16[16,1024]{1,0:T(8,128)(2,1)}) %reduce-scatter.7.cloned.1.call-update) | async-done | bytes 32784 | tf_op jit(solution)/shard_map/reduce_scatter | solution.py:96
  280.2 1.0 convolution_subtract_fusion.4
  281.2 1.0 maximum_select_fusion
  282.3 0.2 all-reduce.15.cloned.1.call-start
  282.5 0.3 fusion.11
  283.0 0.0 collective-permute-start.2
  283.0 2.9 collective-permute-start.3
  286.0 1.6 collective-permute-done.2
  287.6 3.0 collective-permute-start.5
  290.5 1.6 collective-permute-done.4
  292.2 4.5 collective-permute-done.6
  296.7 73.5 %all-reduce.13.cloned.1.call-done = f32[2064,128]{1,0:T(8,128)} async-done(((f32[2064,128]{1,0:T(8,128)}), f32[2064,128]{1,0:T(8,128)}) %all-reduce.13.cloned.1.call-update) | async-done | bytes 1056784 | tf_op jit(solution)/shard_map/psum | solution.py:29
  370.2 2.2 convolution_convert_fusion
  372.4 0.2 fusion.32
  372.6 0.2 fusion.38
  372.8 0.2 convolution_subtract_fusion.2
  373.0 6.7 %convolution_subtract_fusion = bf16[2048,1024]{1,0:T(8,128)(2,1)} fusion(f32[2048,1024]{1,0:T(8,128)} %convolution_subtract_fusion.1, bf16[128,1024]{1,0:T(8,128)(2,1)S(1)} %constant_dynamic-update-slice_fusion, bf16[2064,128]{1,0:T(8,128)(2,1)S(1)} %convolution_convert_fusion), kind=kOutput, calls=%fused_computation.1 | convolution fusion | flops 541065216 | bytes 13369344 | tf_op jit(solution)/shard_map/dot_general | solution.py:117
  379.6 2.0 convolution_add_fusion.1
  381.7 0.0 all-reduce.17.cloned.1.call-start
  381.7 3.6 fusion
  385.3 1.2 fusion.4
  386.6 4.1 slice.97
  390.8 48.5 %all-reduce.15.cloned.1.call-done = f32[128,128]{1,0:T(8,128)} async-done(((f32[128,128]{1,0:T(8,128)}), f32[128,128]{1,0:T(8,128)}) %all-reduce.15.cloned.1.call-update) | async-done | bytes 65552 | tf_op jit(solution)/shard_map/psum | solution.py:85
  439.3 0.6 broadcast_select_fusion
  439.9 0.0 reduce-scatter.9.cloned.1.call-start
  440.0 0.6 pad_maximum_fusion.2
  440.6 0.0 reduce-scatter.9.cloned.1.call-update
  440.7 4.7 pad_maximum_fusion
  445.4 78.0 %all-reduce.17.cloned.1.call-done = f32[128,128]{1,0:T(8,128)} async-done(((f32[128,128]{1,0:T(8,128)}), f32[128,128]{1,0:T(8,128)}) %all-reduce.17.cloned.1.call-update) | async-done | bytes 65552 | tf_op jit(solution)/shard_map/psum | solution.py:29
  523.4 1.1 fusion.1
  524.5 0.3 fusion.43
  524.8 0.2 fusion.24
  525.0 0.1 copy.67
  525.1 30.3 %reduce-scatter.9.cloned.1.call-done = bf16[16,1024]{1,0:T(8,128)(2,1)} async-done(((bf16[128,1024]{1,0:T(8,128)(2,1)}), bf16[16,1024]{1,0:T(8,128)(2,1)}) %reduce-scatter.9.cloned.1.call-update) | async-done | bytes 32784 | tf_op jit(solution)/shard_map/reduce_scatter | solution.py:118
  555.5 1.0 convolution_subtract_fusion.3
  556.5 0.6 pad_maximum_fusion.1
  (51 shorter events, 0.3 us)
Async XLA Ops:
  7.2 94.3 %all-reduce.7.cloned.1.call-start = ((), (), s32[]{:S(2)}) async-start(), calls=%async_computation.2 | async-start | bytes 2097152 | tf_op jit(solution)/shard_map/psum | solution.py:29
  9.5 154.1 %all-reduce.9.cloned.1.call-start = ((), (), s32[]{:S(2)}) async-start(), calls=%async_computation.3 | async-start | bytes 131072 | tf_op jit(solution)/shard_map/psum | solution.py:85
  9.6 273.4 %collective-permute-start = (bf16[16,1024]{1,0:T(8,128)(2,1)}, bf16[16,1024]{1,0:T(8,128)(2,1)S(1)}, u32[]{:S(2)}, u32[]{:S(2)}) collective-permute-start(bf16[16,1024]{1,0:T(8,128)(2,1)} %param.13), channel_id=1, source_target_pairs={{0,16},{16,32},{32,48},{48,64},{64,80},{80,96},{96,112},{112,0},{1... | collective-permute-start | bytes 98312 | tf_op jit(solution)/shard_map/ppermute | solution.py:17
  9.6 273.4 %collective-permute-start.1 = (bf16[16,1024]{1,0:T(8,128)(2,1)}, bf16[16,1024]{1,0:T(8,128)(2,1)S(1)}, u32[]{:S(2)}, u32[]{:S(2)}) collective-permute-start(bf16[16,1024]{1,0:T(8,128)(2,1)} %param.13), channel_id=1, source_target_pairs={{0,112},{16,0},{32,16},{48,32},{64,48},{80,64},{96,80},{112,96},{1... | collective-permute-start | bytes 98312 | tf_op jit(solution)/shard_map/ppermute | solution.py:20
  105.7 142.0 %all-reduce.11.cloned.1.call-start = ((), (), s32[]{:S(2)}) async-start(), calls=%async_computation.4 | async-start | bytes 131072 | tf_op jit(solution)/shard_map/psum | solution.py:29
  113.7 134.1 %copy-start.1 = (f32[128,128]{1,0:T(8,128)S(1)}, f32[128,128]{1,0:T(8,128)}, u32[]{:S(2)}) copy-start(f32[128,128]{1,0:T(8,128)} %param.16) | copy-start | bytes 196612
  113.7 134.1 %copy-start.6 = (f32[128,128]{1,0:T(8,128)S(1)}, f32[128,128]{1,0:T(8,128)}, u32[]{:S(2)}) copy-start(f32[128,128]{1,0:T(8,128)} %param.21) | copy-start | bytes 196612
  113.7 166.6 %copy-start.7 = (f32[16,1024]{1,0:T(8,128)S(1)}, f32[16,1024]{1,0:T(8,128)}, u32[]{:S(2)}) copy-start(f32[16,1024]{1,0:T(8,128)} %param.19) | copy-start | bytes 196612
  164.3 117.0 %slice-start = ((f32[2048,1024]{1,0:T(8,128)}), f32[2048,128]{1,0:T(8,128)S(1)}, s32[]{:S(2)}) async-start(f32[2048,1024]{1,0:T(8,128)} %convolution_subtract_fusion.1), calls=%async_computation.10 | async-start | bytes 2097152 | tf_op jit(solution)/shard_map/slice | solution.py:104
  164.3 116.0 %reduce-scatter.7.cloned.1.call-start = ((), (), s32[]{:S(2)}) async-start(), calls=%async_computation.8 | async-start | bytes 294912 | tf_op jit(solution)/shard_map/reduce_scatter | solution.py:96
  168.0 114.8 %copy-start.10 = (bf16[16,1024]{1,0:T(8,128)(2,1)S(1)}, bf16[16,1024]{1,0:T(8,128)(2,1)}, u32[]{:S(2)}) copy-start(bf16[16,1024]{1,0:T(8,128)(2,1)} %param.13) | copy-start | bytes 98308
  168.0 204.3 %copy-start.3 = (bf16[16,1024]{1,0:T(8,128)(2,1)S(1)}, bf16[16,1024]{1,0:T(8,128)(2,1)}, u32[]{:S(2)}) copy-start(bf16[16,1024]{1,0:T(8,128)(2,1)} %param.14) | copy-start | bytes 98308
  168.1 202.1 %all-reduce.13.cloned.1.call-start = ((), (), s32[]{:S(2)}) async-start(), calls=%async_computation.5 | async-start | bytes 2113536 | tf_op jit(solution)/shard_map/psum | solution.py:29
  249.4 130.3 %copy-start.4 = (f32[128,128]{1,0:T(8,128)}, f32[128,128]{1,0:T(8,128)S(1)}, u32[]{:S(2)}) copy-start(f32[128,128]{1,0:T(8,128)S(1)} %get-tuple-element.16) | copy-start | bytes 196612
  282.3 157.0 %all-reduce.15.cloned.1.call-start = ((), (), s32[]{:S(2)}) async-start(), calls=%async_computation.6 | async-start | bytes 131072 | tf_op jit(solution)/shard_map/psum | solution.py:85
  283.0 4.6 collective-permute-start.2
  283.0 4.5 collective-permute-start.3
  287.6 4.6 collective-permute-start.4
  287.6 4.6 collective-permute-start.5
  292.1 4.6 collective-permute-start.6
  373.0 13.6 %copy-start = (f32[16,1024]{1,0:T(8,128)}, f32[16,1024]{1,0:T(8,128)S(1)}, u32[]{:S(2)}) copy-start(f32[16,1024]{1,0:T(8,128)S(1)} %convolution_subtract_fusion.2) | copy-start | bytes 196612
  381.7 141.7 %all-reduce.17.cloned.1.call-start = ((), (), s32[]{:S(2)}) async-start(), calls=%async_computation.7 | async-start | bytes 131072 | tf_op jit(solution)/shard_map/psum | solution.py:29
  386.6 53.4 %slice-start.1 = ((f32[16,1024]{1,0:T(8,128)}), f32[16,896]{1,0:T(8,128)S(1)}, s32[]{:S(2)}) async-start(f32[16,1024]{1,0:T(8,128)} %copy-done), calls=%async_computation.11 | async-start | bytes 114688 | tf_op jit(solution)/shard_map/slice | solution.py:140
  439.9 115.5 %reduce-scatter.9.cloned.1.call-start = ((), (), s32[]{:S(2)}) async-start(), calls=%async_computation.9 | async-start | bytes 294912 | tf_op jit(solution)/shard_map/reduce_scatter | solution.py:118
  440.7 82.7 %copy-start.2 = (f32[128,128]{1,0:T(8,128)S(1)}, f32[128,128]{1,0:T(8,128)}, u32[]{:S(2)}) copy-start(f32[128,128]{1,0:T(8,128)} %param.15) | copy-start | bytes 196612
  440.7 82.7 %copy-start.8 = (f32[128,128]{1,0:T(8,128)S(1)}, f32[128,128]{1,0:T(8,128)}, u32[]{:S(2)}) copy-start(f32[128,128]{1,0:T(8,128)} %param.20) | copy-start | bytes 196612
  440.7 114.8 %copy-start.9 = (f32[16,1024]{1,0:T(8,128)S(1)}, f32[16,1024]{1,0:T(8,128)}, u32[]{:S(2)}) copy-start(f32[16,1024]{1,0:T(8,128)} %param.18) | copy-start | bytes 196612
  525.0 32.1 %copy-start.5 = (f32[128,128]{1,0:T(8,128)}, f32[128,128]{1,0:T(8,128)S(1)}, u32[]{:S(2)}) copy-start(f32[128,128]{1,0:T(8,128)S(1)} %get-tuple-element.18) | copy-start | bytes 196612
Sparse Core Ops, SparseCore 0:
  11.8 89.6 all-reduce.6
  105.8 57.6 all-reduce.8
  167.7 79.9 all-reduce.10
  250.5 29.6 reduce-scatter.6
  284.3 85.7 all-reduce.12
  381.8 57.4 all-reduce.14
  443.4 79.9 all-reduce.16
  525.7 29.6 reduce-scatter.8
